TPU v7x, 32 devices: a whole 2x2x4 slice. The times are simulated.
32 devices in a mesh: group: 2 (over x), mod: 4 (over y, core), dir: 4 (over z).
Axes of the slice: x: 2, y: 2, z: 4, core: 2. Of those that a mesh axis runs over, the one named last changes fastest.
Arguments:
- screens: float32 [8, 512, 512], P('group', 'mod'), parts along dimension 0, may hold values from -6 to 6
- footprint: int32 [8, 4, 2], P(('group', 'dir')), parts along dimension 0, may hold values from 0 to 191
- fraction: int32 [8, 4, 2], P(('group', 'dir')), parts along dimension 0, may hold values from 0 to 15
- tilt_steps: int32 [16, 2], P(('group', 'mod')), parts along dimension 0, may hold values from -64 to 64
- facet_shift: int32 [4, 2], replicated, may hold values from 80 to 160
Outputs:
- detector: float32 [8, 640, 640], P(('group', 'dir'), 'mod'), parts along dimension 0
There are 2 independent parts, one for each index of `group`. A program takes and returns all parts, laid end to end along the dimension named above; an argument that names none is the same for every part. Nothing has to cross between parts.
All inputs are finite; a program needn't handle non-finite values.
Results may differ from a plain program's by a relative error of at most 0.0055.
Values may be sent and summed in bfloat16 or wider, within the bound.
A program may use at most 64 MiB of HBM per device.

v0:
```python
import functools
import math

import jax
import jax.numpy as jnp
import numpy as np
from jax import lax
from jax.experimental import pallas as pl
from jax.experimental.pallas import tpu as pltpu
from jax.sharding import PartitionSpec as P

P_SIZE = 320
PAD = 640
WIDE = 384
HALF = P_SIZE // 2
MESH = pl.DeviceIdType.MESH
F32 = jnp.float32
BF16 = jnp.bfloat16


def tables(chips, sizes):
    order = np.concatenate([np.arange(0, PAD, 2), np.arange(1, PAD, 2)])

    def parts(first, second, sign):
        turn = np.mod((first - PAD // 2)[:, None] * (second - PAD // 2)[None, :], PAD)
        angle = sign * 2.0 * np.pi / PAD * turn
        return np.cos(angle) / np.sqrt(PAD), np.sin(angle) / np.sqrt(PAD)

    pupil = np.arange(P_SIZE) + (PAD - P_SIZE) // 2
    padded = np.arange(WIDE) + (PAD - P_SIZE) // 2
    d_re, d_im = parts(order, pupil, -1.0)
    left_pupil = np.stack([np.concatenate([d_re, -d_im], 1), np.concatenate([d_im, d_re], 1)])
    keep = (np.arange(WIDE) < P_SIZE)[:, None]
    right_pupil = np.stack([part * keep for part in parts(padded, order, -1.0)])
    upper = np.arange(PAD // 2)
    g_re, g_im = parts(upper, order, 1.0)
    left_focal = []
    for parity in range(2):
        cut = slice(parity * P_SIZE, (parity + 1) * P_SIZE)
        left_focal.append(
            [
                np.concatenate([g_re[:, cut], -g_im[:, cut]], 1),
                np.concatenate([g_im[:, cut], g_re[:, cut]], 1),
            ]
        )
    left_focal = np.asarray(left_focal).reshape(2, 2, chips, sum(sizes), PAD)
    cuts = np.split(left_focal, np.cumsum(sizes)[:-1], axis=3)
    left_focal = np.concatenate([cut.reshape(2, -1, PAD) for cut in cuts], 1)
    right_focal = np.stack(parts(order, np.arange(PAD), 1.0))
    return [np.asarray(t, dtype=BF16) for t in (left_pupil, right_pupil, left_focal, right_focal)]


def turn_parts(steps, period):
    quarter = jnp.round(steps * (4.0 / period))
    rest = (steps - quarter * (period / 4.0)) * (2.0 * math.pi / period)
    return quadrant_parts(rest, quarter.astype(jnp.int32))


def code_parts(code):
    quarter = (code + 8192) >> 14
    rest = (code - (quarter << 14)).astype(F32) * (2.0 * math.pi / 65536)
    return quadrant_parts(rest, quarter)


def wrapped(code):
    return ((code << 16) >> 16).astype(jnp.int16)


def quadrant_parts(rest, index):
    sq = rest * rest
    sine = rest * (1.0 + sq * (-1.0 / 6 + sq * (1.0 / 120 + sq * (-1.0 / 5040 + sq * (1.0 / 362880)))))
    cosine = 1.0 + sq * (-0.5 + sq * (1.0 / 24 + sq * (-1.0 / 720 + sq * (1.0 / 40320))))
    odd = (index & 1) == 1
    cos_out = jnp.where(odd, sine, cosine)
    sin_out = jnp.where(odd, cosine, sine)
    cos_out = jnp.where(((index + 1) & 2) == 2, -cos_out, cos_out)
    sin_out = jnp.where((index & 2) == 2, -sin_out, sin_out)
    return cos_out, sin_out


def iota(shape, axis):
    return lax.broadcasted_iota(jnp.int32, shape, axis)


def dot(left, right):
    return jnp.dot(left, right, preferred_element_type=F32)


def kernel(
    n, sizes, layers, band, points,
    footprint_hbm, fraction_hbm, tilt_hbm, facet_hbm,
    screens_hbm, left_pupil_hbm, right_pupil_hbm, left_focal_hbm, right_focal_hbm,
    out,
    footprint, fraction, tilt, facet, screens,
    lp, rp_in, rp, lf, rf_in, rf,
    own, snd1, rcv1, snd2, rcv2, csnd, crcv,
    modb, mbuf, mk, bk, mask_c, mask_s, both, acc, isnd, ircv, ysnd, yrcv,
    small_sem, load_sem, s1, r1, s2, r2, s3, r3, s4, r4, s5, r5,
):
    m = n // 2
    pieces = len(sizes)
    offsets = [sum(sizes[:i]) for i in range(pieces)]
    part_rows = HALF // 2
    me = lax.axis_index("mod")
    core = lax.rem(me, 2)
    chip = me // 2
    other = 1 - core
    partner = chip * 2 + other

    small = [
        pltpu.make_async_copy(src, dst, small_sem.at[i])
        for i, (src, dst) in enumerate(
            (
                (footprint_hbm, footprint), (fraction_hbm, fraction), (screens_hbm, screens),
                (tilt_hbm, tilt), (facet_hbm, facet),
            )
        )
    ]
    for load in small:
        load.start()
    loads = [
        pltpu.make_async_copy(src, dst, load_sem.at[i])
        for i, (src, dst) in enumerate(
            ((right_pupil_hbm, rp_in), (left_pupil_hbm, lp), (left_focal_hbm, lf), (right_focal_hbm, rf_in))
        )
    ]
    for load in loads:
        load.start()

    barrier = pltpu.get_barrier_semaphore()
    for k in range(1, n):
        pl.semaphore_signal(
            barrier, inc=1, device_id={"mod": lax.rem(me + k, n)}, device_id_type=MESH
        )

    def send(src, dst, send_sem, recv_sem, target):
        return pltpu.make_async_remote_copy(
            src_ref=src, dst_ref=dst, send_sem=send_sem, recv_sem=recv_sem,
            device_id={"mod": target}, device_id_type=MESH,
        )

    for load in small:
        load.wait()
    split = []
    for layer in range(layers):
        frac = fraction[0, 1, layer].astype(F32) / 16.0
        gap = iota((screens.shape[2], WIDE), 0) - iota((screens.shape[2], WIDE), 1) - footprint[0, 1, layer]
        pick = jnp.where(gap == 0, 1.0 - frac, jnp.where(gap == 1, frac, 0.0)).astype(BF16)
        whole = screens[layer]
        high = whole.astype(BF16)
        low = (whole - high.astype(F32)).astype(BF16)
        value = dot(high, pick) + dot(low, pick)
        value_high = value.astype(BF16)
        split.append((value_high, (value - value_high.astype(F32)).astype(BF16)))

    def partial(first):
        total = jnp.zeros((part_rows, WIDE), F32)
        for layer in range(layers):
            frac = fraction[0, 0, layer].astype(F32) / 16.0
            gap = (
                iota((part_rows, band), 1) + me * band
                - iota((part_rows, band), 0) - first - footprint[0, 0, layer]
            )
            pick = jnp.where(gap == 0, 1.0 - frac, jnp.where(gap == 1, frac, 0.0)).astype(BF16)
            total = total + dot(pick, split[layer][0]) + dot(pick, split[layer][1])
        return jnp.round(total * (32768.0 / math.pi)).astype(jnp.int32)

    first = []
    for q in range(2):
        snd1[q] = wrapped(partial(other * HALF + q * part_rows))
        if q == 0:
            pl.semaphore_wait(barrier, n - 1)
        copy = send(snd1.at[q], rcv1.at[q], s1.at[q], r1.at[q], partner)
        copy.start()
        first.append(copy)
    for q in range(2):
        own[q] = partial(core * HALF + q * part_rows)

    def mask_chunk(chunk):
        parity, lower = chunk // 2, chunk % 2
        along_u = 2 * (iota((HALF, 1), 0) + lower * HALF) + parity - PAD // 2
        lane = iota((1, PAD), 1)
        spot = jnp.where(lane < P_SIZE, lane, lane - P_SIZE)
        along_v = jnp.where(lane < P_SIZE, 2 * spot, 2 * spot + 1) - PAD // 2
        right = along_v >= 0
        sign = 2 * lower - 1
        cut = slice(lower * HALF, (lower + 1) * HALF)
        row_shift = sign * jnp.where(right, facet[0, 2 * lower + 1], facet[0, 2 * lower])
        col_shift = jnp.where(right, facet[1, 2 * lower + 1], -facet[1, 2 * lower])
        steps = (
            row_shift.astype(F32) * along_u.astype(F32)
            + (col_shift * along_v).astype(F32)
        )
        cos_part, sin_part = turn_parts(-steps, float(PAD))
        mask_c[parity, cut] = cos_part
        mask_s[parity, cut] = sin_part

    mask_chunk(0)
    second = []
    for q in range(2):
        first[q].wait()
        total = own[q] + rcv1[q].astype(jnp.int32)
        own[q] = total
        snd2[q] = wrapped(total)
        copies = []
        for k in range(1, m):
            copy = send(
                snd2.at[q], rcv2.at[k - 1, q], s2.at[k - 1, q], r2.at[k - 1, q], lax.rem(me + 2 * k, n)
            )
            copy.start()
            copies.append(copy)
        second.append(copies)

    mask_chunk(1)
    mask_chunk(2)
    mask_chunk(3)
    for load in loads:
        load.wait()
    rp[0:WIDE, 0:PAD] = rp_in[0]
    rp[0:WIDE, PAD:] = rp_in[1]
    rp[WIDE:, 0:PAD] = -rp_in[1]
    rp[WIDE:, PAD:] = rp_in[0]
    rf[0:PAD, 0:PAD] = rf_in[0]
    rf[0:PAD, PAD:] = rf_in[1]
    rf[PAD:, 0:PAD] = -rf_in[1]
    rf[PAD:, PAD:] = rf_in[0]

    third = []
    for q in range(2):
        code = own[q]
        for k in range(1, m):
            second[q][k - 1].wait()
            code = code + rcv2[k - 1, q].astype(jnp.int32)
        own[q] = code
        csnd[q] = wrapped(code)
        copy = send(csnd.at[q], crcv.at[q], s3.at[q], r3.at[q], partner)
        copy.start()
        third.append(copy)

    def pupil_stage(codes, which):
        for q in range(2):
            along_y = 2 * (iota((part_rows, 1), 0) + which * HALF + q * part_rows) - P_SIZE + 1
            along_x = 2 * iota((1, WIDE), 1) - P_SIZE + 1
            radius = along_y * along_y + along_x * along_x
            edge = P_SIZE * 28 // 100 * (P_SIZE * 28 // 100)
            inside = (radius <= P_SIZE * P_SIZE) & (radius >= edge)
            cos_part, sin_part = code_parts(codes[q].astype(jnp.int32))
            wide_re = jnp.where(inside, cos_part, 0.0).astype(BF16).astype(F32)
            wide_im = jnp.where(inside, sin_part, 0.0).astype(BF16).astype(F32)
            for p in range(points):
                row_ids = iota((part_rows, 1), 0) + which * HALF + q * part_rows
                row_steps = tilt[p, 0].astype(F32) * row_ids.astype(F32)
                col_steps = tilt[p, 1].astype(F32) * iota((1, WIDE), 1).astype(F32)
                row_c, row_s = turn_parts(row_steps, 8.0 * PAD)
                col_c, col_s = turn_parts(col_steps, 8.0 * PAD)
                tilt_c = row_c * col_c - row_s * col_s
                tilt_s = row_s * col_c + row_c * col_s
                cut = slice(p * HALF + q * part_rows, p * HALF + (q + 1) * part_rows)
                modb[cut, 0:WIDE] = (wide_re * tilt_c - wide_im * tilt_s).astype(BF16)
                modb[cut, WIDE:] = (wide_re * tilt_s + wide_im * tilt_c).astype(BF16)
        start = pl.multiple_of(which * HALF, 32)
        wide = dot(modb[...], rp[...]).astype(BF16)
        for p in range(points):
            cut = slice(p * HALF, (p + 1) * HALF)
            mbuf[pl.ds(start, HALF), p * PAD : (p + 1) * PAD] = wide[cut, :PAD]
            mbuf[pl.ds(start + P_SIZE, HALF), p * PAD : (p + 1) * PAD] = wide[cut, PAD:]

    pupil_stage(own, core)
    for copy in third:
        copy.wait()
    pupil_stage(crcv, other)

    for parity in range(2):
        cut = slice(parity * P_SIZE, (parity + 1) * P_SIZE)
        for p in range(points):
            lanes = slice(p * PAD, (p + 1) * PAD)
            focal_re = dot(lp[0, cut, :], mbuf[:, lanes])
            focal_im = dot(lp[1, cut, :], mbuf[:, lanes])
            mc = mask_c[parity]
            ms = mask_s[parity]
            mk[parity, :P_SIZE, lanes] = (focal_re * mc - focal_im * ms).astype(BF16)
            mk[parity, P_SIZE:, lanes] = (focal_re * ms + focal_im * mc).astype(BF16)

    def focal_stage(piece):
        rows = sizes[piece]
        cut = slice(2 * m * offsets[piece], 2 * m * (offsets[piece] + rows))
        even = dot(lf[0, cut, :], mk[0])
        odd = dot(lf[1, cut, :], mk[1])
        first_row = 2 * points * offsets[piece]
        for sign in range(2):
            value = ((even + odd) if sign == 0 else (even - odd)).astype(BF16)
            for part in range(2):
                for j in range(m):
                    block = j + sign * m
                    base = (part * m + j) * rows
                    for p in range(points):
                        spot = first_row + ((block % 2) * points + p) * rows
                        bk[block // 2, spot : spot + rows, part * PAD : (part + 1) * PAD] = value[
                            base : base + rows, p * PAD : (p + 1) * PAD
                        ]

    def cut_of(piece):
        return slice(offsets[piece], offsets[piece] + sizes[piece])

    waiting = []

    def drain():
        while waiting:
            k, cut, inner = waiting.pop(0)
            inner.wait()
            ysnd[k - 1, cut] = (acc[k, cut] + ircv[k, cut].astype(F32)).astype(BF16)
            spot = len(pending)
            outer = send(
                ysnd.at[k - 1, cut], yrcv.at[k - 1, cut], s5.at[spot], r5.at[spot], lax.rem(me + 2 * k, n)
            )
            outer.start()
            pending.append(outer)

    def image_stage(k, piece):
        rows = sizes[piece]
        cut = cut_of(piece)
        target = lax.rem(chip + k, m)
        first_row = 2 * points * offsets[piece]
        image = dot(bk[target, first_row : first_row + 2 * points * rows, :], rf[...])
        power = image[:, :PAD] * image[:, :PAD] + image[:, PAD:] * image[:, PAD:]
        for half in range(2):
            total = None
            for p in range(points):
                spot = (half * points + p) * rows
                term = power[spot : spot + rows]
                total = term if total is None else total + term
            both[half, cut] = total
        isnd[k, cut] = both[other, cut].astype(BF16)
        acc[k, cut] = both[core, cut]
        inner = send(isnd.at[k, cut], ircv.at[k, cut], s4.at[k, piece], r4.at[k, piece], partner)
        inner.start()
        return inner

    pending = []
    for piece in range(pieces):
        focal_stage(piece)
        for k in range(1, m):
            inner = image_stage(k, piece)
            drain()
            waiting.append((k, cut_of(piece), inner))
    last = []
    for piece in range(pieces):
        last.append(image_stage(0, piece))
        drain()
    for inner in last:
        inner.wait()
    for outer in pending:
        outer.wait()
    total = acc[0] + ircv[0].astype(F32)
    for k in range(1, m):
        total = total + yrcv[k - 1].astype(F32)
    out[0] = total


def solution(mesh):
    n = mesh.shape["mod"]
    m = n // 2
    whole_rows = PAD // n
    units = whole_rows // 16
    if whole_rows % 16 == 0 and units >= 6:
        third = units // 3
        sizes = [16 * (units - 2 * third), 16 * third, 16 * third]
    else:
        sizes = [whole_rows]
    pieces = len(sizes)
    consts = tables(m, sizes)
    part_rows = HALF // 2

    def shards(screens, footprint, fraction, tilt_steps, facet_shift):
        layers, band, width = screens.shape
        points = tilt_steps.shape[0]
        vmem = pl.BlockSpec(memory_space=pltpu.VMEM)
        hbm = pl.BlockSpec(memory_space=pltpu.HBM)
        dma = pltpu.SemaphoreType.DMA
        detector = pl.pallas_call(
            functools.partial(kernel, n, sizes, layers, band, points),
            out_shape=jax.ShapeDtypeStruct((1, whole_rows, PAD), F32),
            in_specs=[hbm] * 9,
            out_specs=vmem,
            scratch_shapes=[
                pltpu.SMEM((1, 2, layers), jnp.int32),
                pltpu.SMEM((1, 2, layers), jnp.int32),
                pltpu.SMEM((points, 2), jnp.int32),
                pltpu.SMEM(facet_shift.shape[::-1], jnp.int32),
                pltpu.VMEM((layers, band, width), F32),
                pltpu.VMEM((2, PAD, PAD), BF16),
                pltpu.VMEM((2, WIDE, PAD), BF16),
                pltpu.VMEM((2 * WIDE, 2 * PAD), BF16),
                pltpu.VMEM((2, 2 * P_SIZE, PAD), BF16),
                pltpu.VMEM((2, PAD, PAD), BF16),
                pltpu.VMEM((2 * PAD, 2 * PAD), BF16),
                pltpu.VMEM((2, part_rows, WIDE), jnp.int32),
                pltpu.VMEM((2, part_rows, WIDE), jnp.int16),
                pltpu.VMEM((2, part_rows, WIDE), jnp.int16),
                pltpu.VMEM((2, part_rows, WIDE), jnp.int16),
                pltpu.VMEM((m - 1, 2, part_rows, WIDE), jnp.int16),
                pltpu.VMEM((2, part_rows, WIDE), jnp.int16),
                pltpu.VMEM((2, part_rows, WIDE), jnp.int16),
                pltpu.VMEM((points * HALF, 2 * WIDE), BF16),
                pltpu.VMEM((PAD, points * PAD), BF16),
                pltpu.VMEM((2, PAD, points * PAD), BF16),
                pltpu.VMEM((m, 2 * points * whole_rows, 2 * PAD), BF16),
                pltpu.VMEM((2, P_SIZE, PAD), F32),
                pltpu.VMEM((2, P_SIZE, PAD), F32),
                pltpu.VMEM((2, whole_rows, PAD), F32),
                pltpu.VMEM((m, whole_rows, PAD), F32),
                pltpu.VMEM((m, whole_rows, PAD), BF16),
                pltpu.VMEM((m, whole_rows, PAD), BF16),
                pltpu.VMEM((m - 1, whole_rows, PAD), BF16),
                pltpu.VMEM((m - 1, whole_rows, PAD), BF16),
                dma((5,)),
                dma((4,)),
                dma((2,)), dma((2,)),
                dma((m - 1, 2)), dma((m - 1, 2)),
                dma((2,)), dma((2,)),
                dma((m, pieces)), dma((m, pieces)),
                dma(((m - 1) * pieces,)), dma(((m - 1) * pieces,)),
            ],
            compiler_params=pltpu.CompilerParams(
                collective_id=0, has_side_effects=True, vmem_limit_bytes=60 * 1024 * 1024
            ),
        )(footprint.swapaxes(1, 2), fraction.swapaxes(1, 2), tilt_steps, facet_shift.T, screens, *[jnp.asarray(t) for t in consts])
        return detector * (4.0 / (points * n))

    placed = (
        P("group", "mod", None),
        P(("group", "dir"), None, None),
        P(("group", "dir"), None, None),
        P(("group", "mod"), None),
        P(),
    )
    return jax.shard_map(
        shards,
        mesh=mesh,
        in_specs=placed,
        out_specs=P(("group", "dir"), "mod", None),
        check_vma=False,
    )
```

profile of v0, /device:TPU:0, one launch (start us, length us, event | category | flops | bytes accessed | tf_op | source)
XLA Modules:
  0.0 30.6 jit_solution(6754462426554348642)
XLA Ops:
  0.0 28.8 %shard_map.91 = f32[1,160,640]{2,1,0:T(8,128)} custom-call(s32[1,2,4]{2,1,0:T(2,128)} %bitcast.3, s32[1,2,4]{2,1,0:T(2,128)} %bitcast.4, s32[2,2]{1,0:T(2,128)} %tilt_hbm.1, s32[2,4]{1,0:T(2,128)} %bitcast.5, f32[4,128,512]{2,1,0:T(8,128)} %screens_hbm.1, bf16[2,640,640]{2,1,0:T(8,128)(2,1)} %constant.10.clone.left_pupil_hbm, ...), custom_call_target="tpu_custom_call" | custom-call | tf_op jit(solution)/shard_map/pallas_call | solution.py:380
  28.8 1.8 %broadcast_multiply_fusion = f32[1,160,640]{2,1,0:T(8,128)} fusion(f32[1,160,640]{2,1,0:T(8,128)} %shard_map.91), kind=kLoop, calls=%fused_computation | loop fusion | flops 102400 | bytes 819200 | tf_op jit(solution)/shard_map/mul | solution.py:428
where the time goes:
time: 30.8 us; the launch traced here: 30.6 us
  Pallas kernels  28.8 us (94%)
  other arithmetic  1.78 us (6%)
    pallas_call x1, Pallas kernels, shards(): pl.pallas_call(functools.partial(kernel, n, sizes, layers, band, points),...  28.8 us
    mul x1, other arithmetic, shards(): return detector * (4.0 / (points * n))  1.78 us

commit v1 on v0

v1 whole, which is shorter than its diff:
```python
import functools
import math

import jax
import jax.numpy as jnp
import numpy as np
from jax import lax
from jax.experimental import pallas as pl
from jax.experimental.pallas import tpu as pltpu
from jax.sharding import PartitionSpec as P

P_SIZE = 320
PAD = 640
LANES = 128
RADIX = PAD // LANES
WIDE = 384
CHUNK = 32
GROUPS = P_SIZE // (2 * CHUNK)
SPLIT = 2 * LANES
MESH = pl.DeviceIdType.MESH
F32 = jnp.float32
BF16 = jnp.bfloat16
C1, C2 = math.cos(0.4 * math.pi), math.cos(0.8 * math.pi)
S1, S2 = math.sin(0.4 * math.pi), math.sin(0.8 * math.pi)


def tables():
    q, b = np.arange(LANES)[:, None], np.arange(LANES)[None, :]
    rows = []
    for s in range(RADIX):
        angle = 2.0 * np.pi / PAD * np.mod(b * (RADIX * q + s), PAD)
        re, im = np.cos(angle) / np.sqrt(PAD), np.sin(angle) / np.sqrt(PAD)
        rows.append(np.concatenate([np.concatenate([re, im], 1), np.concatenate([-im, re], 1)], 0))
    table = np.stack(rows)
    return [np.asarray(t, dtype=BF16) for t in (table, table.transpose(0, 2, 1))]


def turn_parts(steps, period):
    quarter = jnp.round(steps * (4.0 / period))
    rest = (steps - quarter * (period / 4.0)) * (2.0 * math.pi / period)
    return quadrant_parts(rest, quarter.astype(jnp.int32))


def code_parts(code):
    quarter = (code + 8192) >> 14
    rest = (code - (quarter << 14)).astype(F32) * (2.0 * math.pi / 65536)
    return quadrant_parts(rest, quarter)


def wrapped(code):
    return ((code << 16) >> 16).astype(jnp.int16)


def quadrant_parts(rest, index):
    sq = rest * rest
    sine = rest * (1.0 + sq * (-1.0 / 6 + sq * (1.0 / 120 + sq * (-1.0 / 5040 + sq * (1.0 / 362880)))))
    cosine = 1.0 + sq * (-0.5 + sq * (1.0 / 24 + sq * (-1.0 / 720 + sq * (1.0 / 40320))))
    odd = (index & 1) == 1
    cos_out = jnp.where(odd, sine, cosine)
    sin_out = jnp.where(odd, cosine, sine)
    cos_out = jnp.where(((index + 1) & 2) == 2, -cos_out, cos_out)
    sin_out = jnp.where((index & 2) == 2, -sin_out, sin_out)
    return cos_out, sin_out


def iota(shape, axis):
    return lax.broadcasted_iota(jnp.int32, shape, axis)


def dot(left, right):
    return jnp.dot(left, right, preferred_element_type=F32)


def times(a, b):
    return a[0] * b[0] - a[1] * b[1], a[0] * b[1] + a[1] * b[0]


def spread(x):
    (x0r, x0i), (x1r, x1i), (x2r, x2i) = x
    out = [None] * RADIX
    out[0] = (x0r + x1r + x2r, x0i + x1i + x2i)
    pr, pi = x0r + C1 * x1r + C2 * x2r, x0i + C1 * x1i + C2 * x2i
    qr, qi = S1 * x1r + S2 * x2r, S1 * x1i + S2 * x2i
    out[1], out[4] = (pr + qi, pi - qr), (pr - qi, pi + qr)
    pr, pi = x0r + C2 * x1r + C1 * x2r, x0i + C2 * x1i + C1 * x2i
    qr, qi = S2 * x1r - S1 * x2r, S2 * x1i - S1 * x2i
    out[2], out[3] = (pr + qi, pi - qr), (pr - qi, pi + qr)
    return out


def spread_two(x):
    (x0r, x0i), (x1r, x1i) = x
    out = [None] * RADIX
    out[0] = (x0r + x1r, x0i + x1i)
    pr, pi, qr, qi = x0r + C1 * x1r, x0i + C1 * x1i, S1 * x1r, S1 * x1i
    out[1], out[4] = (pr + qi, pi - qr), (pr - qi, pi + qr)
    pr, pi, qr, qi = x0r + C2 * x1r, x0i + C2 * x1i, S2 * x1r, S2 * x1i
    out[2], out[3] = (pr + qi, pi - qr), (pr - qi, pi + qr)
    return out


def gather_blocks(z, wanted):
    t1 = [z[1][k] + z[4][k] for k in range(2)]
    t2 = [z[2][k] + z[3][k] for k in range(2)]
    t3 = [z[1][k] - z[4][k] for k in range(2)]
    t4 = [z[2][k] - z[3][k] for k in range(2)]
    out = {0: tuple(z[0][k] + t1[k] + t2[k] for k in range(2))}
    if 1 in wanted or 4 in wanted:
        a = [z[0][k] + C1 * t1[k] + C2 * t2[k] for k in range(2)]
        b = [S1 * t3[k] + S2 * t4[k] for k in range(2)]
        out[1] = (a[0] - b[1], a[1] + b[0])
        out[4] = (a[0] + b[1], a[1] - b[0])
    if 2 in wanted or 3 in wanted:
        a = [z[0][k] + C2 * t1[k] + C1 * t2[k] for k in range(2)]
        b = [S2 * t3[k] - S1 * t4[k] for k in range(2)]
        out[2] = (a[0] - b[1], a[1] + b[0])
        out[3] = (a[0] + b[1], a[1] - b[0])
    return [out[k] for k in wanted]


def kernel(
    n, layers, band, points, skip,
    footprint_hbm, fraction_hbm, tilt_hbm, facet_hbm,
    screens_hbm, table_hbm, flipped_hbm,
    out,
    footprint, fraction, tilts, facet, screens, table, flipped,
    pick, high, low, own, snd1, rcv1, snd2, rcv2, csnd, crcv,
    col_c, col_s, base_c, base_s, step_c, step_s, mask_c, mask_s,
    half, back, acc, isnd, ircv,
    small_sem, load_sem, st, rt, s1, r1, s2, r2, s3, r3, s4, r4,
):
    m = n // 2
    total_points = points * m
    rows_out = PAD // m
    sends = GROUPS - 1 if skip else GROUPS
    me = lax.axis_index("mod")
    core = lax.rem(me, 2)
    chip = me // 2
    other = 1 - core
    partner = chip * 2 + other
    start = chip if skip else 0

    small = [
        pltpu.make_async_copy(src, dst, small_sem.at[i])
        for i, (src, dst) in enumerate(
            ((footprint_hbm, footprint), (fraction_hbm, fraction), (facet_hbm, facet), (tilt_hbm, tilts.at[0]))
        )
    ]
    loads = [
        pltpu.make_async_copy(src, dst, load_sem.at[i])
        for i, (src, dst) in enumerate(((screens_hbm, screens), (table_hbm, table), (flipped_hbm, flipped)))
    ]
    for load in small + loads:
        load.start()

    barrier = pltpu.get_barrier_semaphore()
    peers = [partner] + [lax.rem(me + 2 * k, n) for k in range(1, m)]
    for peer in peers:
        pl.semaphore_signal(barrier, inc=1, device_id={"mod": peer}, device_id_type=MESH)

    def send(src, dst, send_sem, recv_sem, target):
        return pltpu.make_async_remote_copy(
            src_ref=src, dst_ref=dst, send_sem=send_sem, recv_sem=recv_sem,
            device_id={"mod": target}, device_id_type=MESH,
        )

    for load in small[:3]:
        load.wait()
    depth = layers * band
    lane = iota((1, depth), 1)
    first_row = jnp.zeros((1, depth), jnp.int32)
    weight = jnp.zeros((1, depth), F32)
    for layer in range(layers):
        here = (lane >= layer * band) & (lane < (layer + 1) * band)
        first_row = jnp.where(here, me * band - layer * band - footprint[0, 0, layer], first_row)
        weight = jnp.where(here, fraction[0, 0, layer].astype(F32) / 16.0, weight)
    place = lane + first_row
    for which in range(2):
        owner = other if which == 0 else core
        for t in range(sends):
            row = iota((CHUNK, 1), 0) + (2 * (start + t) + owner) * CHUNK
            gap = place - row
            chosen = jnp.where(gap == 0, 1.0 - weight, jnp.where(gap == 1, weight, 0.0))
            pick[which, t * CHUNK : (t + 1) * CHUNK, :] = chosen.astype(BF16)

    loads[0].wait()
    lanes = iota((1, LANES), 1)
    for layer in range(layers):
        col = footprint[0, 1, layer]
        far = col >= LANES
        near = col & (LANES - 1)
        frac = fraction[0, 1, layer].astype(F32) / 16.0
        slabs = [screens[layer, :, j * LANES : (j + 1) * LANES] for j in range(4)]
        slabs = [jnp.where(far, slabs[min(j + 1, 3)], slabs[j]) for j in range(4)]
        turn = (LANES - near) & (LANES - 1)
        rolled = [pltpu.roll(slab, turn, 1) for slab in slabs]
        nexts = [pltpu.roll(slab, LANES - 1, 1) for slab in rolled]
        for j in range(3):
            this = jnp.where(lanes < LANES - near, rolled[j], rolled[j + 1])
            after = jnp.where(lanes < LANES - 1 - near, nexts[j], nexts[j + 1])
            value = (1.0 - frac) * this + frac * after
            value_high = value.astype(BF16)
            cut = (slice(layer * band, (layer + 1) * band), slice(j * LANES, (j + 1) * LANES))
            high[cut] = value_high
            low[cut] = (value - value_high.astype(F32)).astype(BF16)

    def partial(which):
        value = dot(pick[which], high[...]) + dot(pick[which], low[...])
        return jnp.round(value * (32768.0 / math.pi)).astype(jnp.int32)

    code = partial(0)
    for t in range(sends):
        snd1[t] = wrapped(code[t * CHUNK : (t + 1) * CHUNK])
    small[3].wait()
    pl.semaphore_wait(barrier, len(peers))
    first = []
    for t in range(sends):
        copy = send(snd1.at[t], rcv1.at[t], s1.at[t], r1.at[t], partner)
        copy.start()
        first.append(copy)
    gather = []
    for k in range(1, m):
        copy = send(tilts.at[0], tilts.at[k], st.at[k - 1], rt.at[k - 1], lax.rem(me + 2 * k, n))
        copy.start()
        gather.append(copy)
    code = partial(1)
    for t in range(sends):
        own[1 + t] = code[t * CHUNK : (t + 1) * CHUNK]
    own[0] = jnp.zeros((CHUNK, WIDE), jnp.int32)
    own[1 + sends] = jnp.zeros((CHUNK, WIDE), jnp.int32)

    def focal_mask(s):
        spot = iota((LANES, LANES), 0)
        lane = iota((LANES, LANES), 1)
        upper, right = spot < LANES // 2, lane < LANES // 2
        along_u = RADIX * spot + s - jnp.where(upper, 0, PAD)
        shift = jnp.where(
            upper,
            jnp.where(right, facet[0, 3], facet[0, 2]),
            jnp.where(right, -facet[0, 1], -facet[0, 0]),
        )
        coef = chip * rows_out - P_SIZE // 2 - shift
        row = turn_parts((coef * along_u).astype(F32), float(PAD))
        for t in range(RADIX):
            along_v = RADIX * iota((8, LANES), 1) + t
            right = iota((8, LANES), 1) < LANES // 2
            along_v = along_v - jnp.where(right, 0, PAD)
            upper = iota((8, LANES), 0) < 4
            shift = jnp.where(
                upper,
                jnp.where(right, facet[1, 3], -facet[1, 2]),
                jnp.where(right, facet[1, 1], -facet[1, 0]),
            )
            coef = -(P_SIZE // 2) - shift
            col_cos, col_sin = turn_parts((coef * along_v).astype(F32), float(PAD))
            for h in range(2):
                rows = slice(h * (LANES // 2), (h + 1) * (LANES // 2))
                pair = (col_cos[4 * h : 4 * h + 1], col_sin[4 * h : 4 * h + 1])
                re, im = times((row[0][rows], row[1][rows]), pair)
                mask_c[s, rows, t * LANES : (t + 1) * LANES] = re
                mask_s[s, rows, t * LANES : (t + 1) * LANES] = im

    focal_mask(0)
    second = []
    for t in range(sends):
        first[t].wait()
        total = own[1 + t] + rcv1[t].astype(jnp.int32)
        own[1 + t] = total
        snd2[t] = wrapped(total)
        copies = []
        for k in range(1, m):
            copy = send(
                snd2.at[t], rcv2.at[k - 1, t], s2.at[k - 1, t], r2.at[k - 1, t], lax.rem(me + 2 * k, n)
            )
            copy.start()
            copies.append(copy)
        second.append(copies)
    for s in range(1, RADIX):
        focal_mask(s)

    for load in loads[1:]:
        load.wait()
    for copy in gather:
        copy.wait()
    for k in range(m):
        for q in range(points):
            p = k * points + q
            steps = tilts[k, q : q + 1, :].astype(F32)
            down, along = steps[:, 0:1], steps[:, 1:2]
            across = along * iota((1, WIDE), 1).astype(F32)
            col_c[p : p + 1, :], col_s[p : p + 1, :] = turn_parts(across, 8.0 * PAD)
            base_c[p], base_s[p] = turn_parts(down * iota((CHUNK, LANES), 0).astype(F32), 8.0 * PAD)
            step_c[p], step_s[p] = turn_parts(
                down * (CHUNK * iota((16, LANES), 0)).astype(F32), 8.0 * PAD
            )

    def pupil_piece(code, which):
        cos_part, sin_part = code_parts(code)
        along_y = 2 * (iota((CHUNK, 1), 0) + which * CHUNK) - P_SIZE + 1
        along_x = 2 * iota((1, WIDE), 1) - P_SIZE + 1
        radius = along_y * along_y + along_x * along_x
        edge = P_SIZE * 28 // 100 * (P_SIZE * 28 // 100)
        inside = (radius <= P_SIZE * P_SIZE) & (radius >= edge)
        field = (jnp.where(inside, cos_part, 0.0), jnp.where(inside, sin_part, 0.0))
        parts = [[] for _ in range(RADIX)]
        for p in range(total_points):
            step = (step_c[p, pl.ds(which, 1), :], step_s[p, pl.ds(which, 1), :])
            blocks = []
            for j in range(3):
                cut = slice(j * LANES, (j + 1) * LANES)
                col = times(step, (col_c[p : p + 1, cut], col_s[p : p + 1, cut]))
                tilt = times((base_c[p], base_s[p]), col)
                blocks.append(times((field[0][:, cut], field[1][:, cut]), tilt))
            for s, pair in enumerate(spread(blocks)):
                parts[s].append(jnp.concatenate(pair, 1).astype(BF16))
        start_row = pl.multiple_of(which * CHUNK, CHUNK)
        for s in range(RADIX):
            wide = dot(jnp.concatenate(parts[s], 0), flipped[s])
            for p in range(total_points):
                half[p, pl.ds(start_row, CHUNK), s * SPLIT : (s + 1) * SPLIT] = wide[
                    p * CHUNK : (p + 1) * CHUNK
                ]

    shift = 1 - 2 * chip if skip else 0
    third = []
    groups = []

    def finish(step, code, group):
        csnd[step] = wrapped(code)
        copy = send(csnd.at[step], crcv.at[step], s3.at[step], r3.at[step], partner)
        copy.start()
        third.append(copy)
        groups.append(group)
        pupil_piece(code, 2 * group + core)

    def take(step):
        third[step].wait()
        pupil_piece(crcv[step].astype(jnp.int32), 2 * groups[step] + other)

    if skip:
        finish(0, own[1 + 3 * chip], chip * (GROUPS - 1))
    for t in range(sends):
        code = own[1 + t + shift]
        for k in range(1, m):
            second[t][k - 1].wait()
            code = code + rcv2[k - 1, t].astype(jnp.int32)
        step = len(third)
        finish(step, code, (1 - start if skip else 0) + t)
        if step > 0:
            take(step - 1)
    take(len(third) - 1)

    owned = rows_out // 2
    slab = acc.shape[1]
    count = owned // slab
    blocks = -(-rows_out // LANES)

    def store_back(p, s, block, pair):
        low_row, high_row = block * LANES, min((block + 1) * LANES, rows_out)
        row = low_row
        while row < high_row:
            piece = row // slab
            stop = min((piece + 1) * slab, high_row)
            where = slice(p * slab + row - piece * slab, p * slab + stop - piece * slab)
            for k in range(2):
                lanes = slice(s * SPLIT + k * LANES, s * SPLIT + (k + 1) * LANES)
                back[piece, where, lanes] = pair[k][row - low_row : stop - low_row].astype(back.dtype)
            row = stop

    def focal_tile(tile):
        mid = P_SIZE - 2 * LANES
        top, bottom = [], []
        for p, s in tile:
            def part(first, last, k):
                return half[p, first:last, s * SPLIT + k * LANES : s * SPLIT + (k + 1) * LANES]
            def pairs(first, last, count):
                return [
                    tuple(part(j * LANES + first, j * LANES + last, k) for k in range(2)) for j in range(count)
                ]
            top.append(spread(pairs(0, mid, 3)))
            bottom.append(spread_two(pairs(mid, LANES, 2)))
        z = []
        for s in range(RADIX):
            stacked = []
            for k in range(2):
                for rows in (top, bottom):
                    stacked.append(
                        jnp.concatenate([rows[i][s][k].astype(BF16) for i in range(len(tile))], 1)
                    )
            focal = dot(table[s], jnp.concatenate(stacked, 0))
            mask = tuple(
                jnp.concatenate([ref[s, :, t * LANES : (t + 1) * LANES] for _, t in tile], 1)
                for ref in (mask_c, mask_s)
            )
            masked = times((focal[:LANES], focal[LANES:]), mask)
            masked = jnp.concatenate([part.astype(BF16) for part in masked], 0)
            value = dot(flipped[s], masked)
            z.append((value[:LANES], value[LANES:]))
        for block, pair in enumerate(gather_blocks(z, list(range(blocks)))):
            for i, (p, s) in enumerate(tile):
                cut = slice(i * LANES, (i + 1) * LANES)
                store_back(p, s, block, (pair[0][:, cut], pair[1][:, cut]))

    todo = [(p, s) for p in range(total_points) for s in range(RADIX)]
    for i in range(0, len(todo), 2):
        focal_tile(todo[i : i + 2])

    def image_piece(owner, c):
        rows = back.at[owner * count + c]
        z = []
        for s in range(RADIX):
            value = dot(rows[:, s * SPLIT : (s + 1) * SPLIT].astype(BF16), table[s])
            z.append((value[:, :LANES], value[:, LANES:]))
        sums = []
        for re, im in gather_blocks(z, list(range(RADIX))):
            power = re * re + im * im
            total = power[:slab]
            for p in range(1, total_points):
                total = total + power[p * slab : (p + 1) * slab]
            sums.append(total)
        return sums

    fourth = []
    for c in range(count):
        for j, block in enumerate(image_piece(other, c)):
            isnd[c, :, j * LANES : (j + 1) * LANES] = block
        copy = send(isnd.at[c], ircv.at[c], s4.at[c], r4.at[c], partner)
        copy.start()
        fourth.append(copy)
    for c in range(count):
        for j, block in enumerate(image_piece(core, c)):
            acc[c, :, j * LANES : (j + 1) * LANES] = block
    for c in range(count):
        fourth[c].wait()
        out[0, c * slab : (c + 1) * slab, :] = acc[c] + ircv[c]


def solution(mesh):
    n = mesh.shape["mod"]
    m = n // 2
    owned = PAD // n
    slab = 80 if owned % 80 == 0 else owned
    consts = tables()

    def shards(screens, footprint, fraction, tilt_steps, facet_shift):
        layers, band, width = screens.shape
        points = tilt_steps.shape[0]
        total = points * m
        reach = 2 * CHUNK * (GROUPS - 1)
        skip = m == 2 and 2 * band <= reach and 2 * band - (width - P_SIZE) >= P_SIZE - reach
        sends = GROUPS - 1 if skip else GROUPS
        vmem = pl.BlockSpec(memory_space=pltpu.VMEM)
        hbm = pl.BlockSpec(memory_space=pltpu.HBM)
        dma = pltpu.SemaphoreType.DMA
        codes = lambda count, kind: pltpu.VMEM((count, CHUNK, WIDE), kind)
        detector = pl.pallas_call(
            functools.partial(kernel, n, layers, band, points, skip),
            out_shape=jax.ShapeDtypeStruct((1, owned, PAD), F32),
            in_specs=[hbm] * 7,
            out_specs=vmem,
            scratch_shapes=[
                pltpu.SMEM((1, 2, layers), jnp.int32),
                pltpu.SMEM((1, 2, layers), jnp.int32),
                pltpu.VMEM((m, points, 2), jnp.int32),
                pltpu.SMEM(facet_shift.shape[::-1], jnp.int32),
                pltpu.VMEM((layers, band, width), F32),
                pltpu.VMEM((RADIX, SPLIT, SPLIT), BF16),
                pltpu.VMEM((RADIX, SPLIT, SPLIT), BF16),
                pltpu.VMEM((2, sends * CHUNK, layers * band), BF16),
                pltpu.VMEM((layers * band, WIDE), BF16),
                pltpu.VMEM((layers * band, WIDE), BF16),
                codes(sends + 2, jnp.int32),
                codes(sends, jnp.int16),
                codes(sends, jnp.int16),
                codes(sends, jnp.int16),
                pltpu.VMEM((m - 1, sends, CHUNK, WIDE), jnp.int16),
                codes(GROUPS, jnp.int16),
                codes(GROUPS, jnp.int16),
                pltpu.VMEM((total, WIDE), F32),
                pltpu.VMEM((total, WIDE), F32),
                pltpu.VMEM((total, CHUNK, LANES), F32),
                pltpu.VMEM((total, CHUNK, LANES), F32),
                pltpu.VMEM((total, 16, LANES), F32),
                pltpu.VMEM((total, 16, LANES), F32),
                pltpu.VMEM((RADIX, LANES, PAD), F32),
                pltpu.VMEM((RADIX, LANES, PAD), F32),
                pltpu.VMEM((total, P_SIZE, 2 * PAD), F32),
                pltpu.VMEM((2 * owned // slab, total * slab, 2 * PAD), BF16 if slab % 16 == 0 else F32),
                pltpu.VMEM((owned // slab, slab, PAD), F32),
                pltpu.VMEM((owned // slab, slab, PAD), F32),
                pltpu.VMEM((owned // slab, slab, PAD), F32),
                dma((4,)),
                dma((3,)),
                dma((m - 1,)), dma((m - 1,)),
                dma((sends,)), dma((sends,)),
                dma((m - 1, sends)), dma((m - 1, sends)),
                dma((GROUPS,)), dma((GROUPS,)),
                dma((owned // slab,)), dma((owned // slab,)),
            ],
            compiler_params=pltpu.CompilerParams(
                collective_id=0, has_side_effects=True, vmem_limit_bytes=60 * 1024 * 1024
            ),
        )(footprint.swapaxes(1, 2), fraction.swapaxes(1, 2), tilt_steps, facet_shift.T, screens, *[jnp.asarray(t) for t in consts])
        return detector * (4.0 / (points * n))

    placed = (
        P("group", "mod", None),
        P(("group", "dir"), None, None),
        P(("group", "dir"), None, None),
        P(("group", "mod"), None),
        P(),
    )
    return jax.shard_map(
        shards,
        mesh=mesh,
        in_specs=placed,
        out_specs=P(("group", "dir"), "mod", None),
        check_vma=False,
    )
```

time: 30.8 us -> 24.9 us (0.81)
  Pallas kernels: 28.8 us -> 22.9 us
    pallas_call x1, Pallas kernels: 28.8 us -> 22.9 us  [shards(): pl.pallas_call(functools.partial(kernel, n, layers, band, points, skip),...]
where the time goes in v1:
time: 24.9 us; the launch traced here: 24.7 us
  Pallas kernels  22.9 us (92%)
  other arithmetic  1.78 us (7%)
    pallas_call x1, Pallas kernels, shards(): pl.pallas_call(functools.partial(kernel, n, layers, band, points, skip),...  22.9 us
    mul x1, other arithmetic, shards(): return detector * (4.0 / (points * n))  1.78 us

profile of v1, /device:TPU:0, one launch (start us, length us, event | category | flops | bytes accessed | tf_op | source)
XLA Modules:
  0.0 24.7 jit_solution(17408279740424616573)
XLA Ops:
  0.0 22.9 %shard_map.73 = f32[1,160,640]{2,1,0:T(8,128)} custom-call(s32[1,2,4]{2,1,0:T(2,128)} %bitcast.3, s32[1,2,4]{2,1,0:T(2,128)} %bitcast.4, s32[2,2]{1,0:T(2,128)} %tilt_hbm.1, s32[2,4]{1,0:T(2,128)} %bitcast.5, f32[4,128,512]{2,1,0:T(8,128)} %screens_hbm.1, bf16[5,256,256]{2,1,0:T(8,128)(2,1)} %constant.6.clone.table_hbm, ...), custom_call_target="tpu_custom_call" | custom-call | tf_op jit(solution)/shard_map/pallas_call | solution.py:456
  22.9 1.8 %broadcast_multiply_fusion = f32[1,160,640]{2,1,0:T(8,128)} fusion(f32[1,160,640]{2,1,0:T(8,128)} %shard_map.73), kind=kLoop, calls=%fused_computation | loop fusion | flops 102400 | bytes 819200 | tf_op jit(solution)/shard_map/mul | solution.py:504

commit v2 on v1

v2 whole, which is shorter than its diff:
```python
import functools
import math

import jax
import jax.numpy as jnp
import numpy as np
from jax import lax
from jax.experimental import pallas as pl
from jax.experimental.pallas import tpu as pltpu
from jax.sharding import PartitionSpec as P

P_SIZE = 320
PAD = 640
LANES = 128
RADIX = PAD // LANES
WIDE = 384
CHUNK = 32
GROUPS = P_SIZE // (2 * CHUNK)
SPLIT = 2 * LANES
MESH = pl.DeviceIdType.MESH
F32 = jnp.float32
BF16 = jnp.bfloat16
SINE = (9.99999604e-01, -1.66665534e-01, 8.33240745e-03, -1.98087363e-04, 2.69981853e-06, -2.03660579e-08)
COSINE = (9.99999221e-01, -4.99994267e-01, 4.16598211e-02, -1.38589124e-03, 2.42043555e-05, -2.19786764e-07)
KEEP = math.sqrt(5.0) / 4.0
S1, S2 = math.sin(0.4 * math.pi), math.sin(0.8 * math.pi)


def tables():
    q, b = np.arange(LANES)[:, None], np.arange(LANES)[None, :]
    rows = []
    for s in range(RADIX):
        angle = 2.0 * np.pi / PAD * np.mod(b * (RADIX * q + s), PAD)
        re, im = np.cos(angle) / np.sqrt(PAD), np.sin(angle) / np.sqrt(PAD)
        rows.append(np.concatenate([np.concatenate([re, im], 1), np.concatenate([-im, re], 1)], 0))
    table = np.stack(rows)
    return [np.asarray(t, dtype=BF16) for t in (table, table.transpose(0, 2, 1))]


def turn_parts(steps, period):
    quarter = jnp.round(steps * (4.0 / period))
    rest = (steps - quarter * (period / 4.0)) * (2.0 * math.pi / period)
    return quadrant_parts(rest, quarter.astype(jnp.int32))


def code_parts(code):
    turn = ((code << 16) >> 16).astype(F32) * (math.pi / 32768)
    sq = turn * turn
    sine, cosine = SINE[-1] * sq + SINE[-2], COSINE[-1] * sq + COSINE[-2]
    for factor in SINE[-3::-1]:
        sine = sine * sq + factor
    for factor in COSINE[-3::-1]:
        cosine = cosine * sq + factor
    return cosine, turn * sine


def wrapped(code):
    return ((code << 16) >> 16).astype(jnp.int16)


def quadrant_parts(rest, index):
    sq = rest * rest
    sine = rest * (1.0 + sq * (-1.0 / 6 + sq * (1.0 / 120 + sq * (-1.0 / 5040 + sq * (1.0 / 362880)))))
    cosine = 1.0 + sq * (-0.5 + sq * (1.0 / 24 + sq * (-1.0 / 720 + sq * (1.0 / 40320))))
    odd = (index & 1) == 1
    cos_out = jnp.where(odd, sine, cosine)
    sin_out = jnp.where(odd, cosine, sine)
    cos_out = jnp.where(((index + 1) & 2) == 2, -cos_out, cos_out)
    sin_out = jnp.where((index & 2) == 2, -sin_out, sin_out)
    return cos_out, sin_out


def iota(shape, axis):
    return lax.broadcasted_iota(jnp.int32, shape, axis)


def dot(left, right):
    return jnp.dot(left, right, preferred_element_type=F32)


def times(a, b):
    return a[0] * b[0] - a[1] * b[1], a[0] * b[1] + a[1] * b[0]


def spread(x):
    if len(x) == 2:
        near = [(x[0][k] - 0.25 * x[1][k], KEEP * x[1][k]) for k in range(2)]
        first = [x[0][k] + x[1][k] for k in range(2)]
        q1 = [S1 * x[1][k] for k in range(2)]
        q2 = [S2 * x[1][k] for k in range(2)]
    else:
        both = [x[1][k] + x[2][k] for k in range(2)]
        near = [(x[0][k] - 0.25 * both[k], KEEP * (x[1][k] - x[2][k])) for k in range(2)]
        first = [x[0][k] + both[k] for k in range(2)]
        q1 = [S1 * x[1][k] + S2 * x[2][k] for k in range(2)]
        q2 = [S2 * x[1][k] - S1 * x[2][k] for k in range(2)]
    p1 = [w + v for w, v in near]
    p2 = [w - v for w, v in near]
    return [
        tuple(first),
        (p1[0] + q1[1], p1[1] - q1[0]),
        (p2[0] + q2[1], p2[1] - q2[0]),
        (p2[0] - q2[1], p2[1] + q2[0]),
        (p1[0] - q1[1], p1[1] + q1[0]),
    ]


def gather_blocks(z, wanted):
    t1 = [z[1][k] + z[4][k] for k in range(2)]
    t2 = [z[2][k] + z[3][k] for k in range(2)]
    t3 = [z[1][k] - z[4][k] for k in range(2)]
    t4 = [z[2][k] - z[3][k] for k in range(2)]
    both = [t1[k] + t2[k] for k in range(2)]
    near = [(z[0][k] - 0.25 * both[k], KEEP * (t1[k] - t2[k])) for k in range(2)]
    p1 = [w + v for w, v in near]
    p2 = [w - v for w, v in near]
    q1 = [S1 * t3[k] + S2 * t4[k] for k in range(2)]
    q2 = [S2 * t3[k] - S1 * t4[k] for k in range(2)]
    out = [
        tuple(z[0][k] + both[k] for k in range(2)),
        (p1[0] - q1[1], p1[1] + q1[0]),
        (p2[0] - q2[1], p2[1] + q2[0]),
        (p2[0] + q2[1], p2[1] - q2[0]),
        (p1[0] + q1[1], p1[1] - q1[0]),
    ]
    return [out[k] for k in wanted]


def kernel(
    n, layers, band, points, skip,
    footprint_hbm, fraction_hbm, tilt_hbm, facet_hbm,
    screens_hbm, table_hbm, flipped_hbm,
    out,
    footprint, fraction, tilts, facet, screens, table, flipped,
    pick, high, low, own, snd1, rcv1, snd2, rcv2, csnd, crcv,
    tilt_c, tilt_s, mask_c, mask_s,
    half, work_a, work_b, masked_a, masked_b, blocks_a, blocks_b, wide, back, acc, isnd, ircv,
    small_sem, load_sem, st, rt, s1, r1, s2, r2, s3, r3, s4, r4,
):
    m = n // 2
    total_points = points * m
    rows_out = PAD // m
    sends = GROUPS - 1 if skip else GROUPS
    me = lax.axis_index("mod")
    core = lax.rem(me, 2)
    chip = me // 2
    other = 1 - core
    partner = chip * 2 + other
    start = chip if skip else 0

    small = [
        pltpu.make_async_copy(src, dst, small_sem.at[i])
        for i, (src, dst) in enumerate(
            ((footprint_hbm, footprint), (fraction_hbm, fraction), (facet_hbm, facet), (tilt_hbm, tilts.at[0]))
        )
    ]
    loads = [
        pltpu.make_async_copy(src, dst, load_sem.at[i])
        for i, (src, dst) in enumerate(((screens_hbm, screens), (table_hbm, table), (flipped_hbm, flipped)))
    ]
    for load in small + loads:
        load.start()

    barrier = pltpu.get_barrier_semaphore()
    peers = [partner] + [lax.rem(me + 2 * k, n) for k in range(1, m)]
    for peer in peers:
        pl.semaphore_signal(barrier, inc=1, device_id={"mod": peer}, device_id_type=MESH)

    def send(src, dst, send_sem, recv_sem, target):
        return pltpu.make_async_remote_copy(
            src_ref=src, dst_ref=dst, send_sem=send_sem, recv_sem=recv_sem,
            device_id={"mod": target}, device_id_type=MESH,
        )

    for load in small[:3]:
        load.wait()
    depth = layers * band
    lane = iota((1, depth), 1)
    first_row = jnp.zeros((1, depth), jnp.int32)
    weight = jnp.zeros((1, depth), F32)
    for layer in range(layers):
        here = (lane >= layer * band) & (lane < (layer + 1) * band)
        first_row = jnp.where(here, me * band - layer * band - footprint[0, 0, layer], first_row)
        weight = jnp.where(here, fraction[0, 0, layer].astype(F32) / 16.0, weight)
    place = lane + first_row
    for which in range(2):
        owner = other if which == 0 else core
        for t in range(sends):
            row = iota((CHUNK, 1), 0) + (2 * (start + t) + owner) * CHUNK
            gap = place - row
            chosen = jnp.where(gap == 0, 1.0 - weight, jnp.where(gap == 1, weight, 0.0))
            pick[which, t * CHUNK : (t + 1) * CHUNK, :] = chosen.astype(BF16)

    def row_factor(rows, along):
        right = iota((rows, LANES), 1) < LANES // 2
        upper = iota((rows, LANES), 0) < rows // 2
        shift = jnp.where(
            upper,
            jnp.where(right, facet[0, 3], facet[0, 2]),
            jnp.where(right, -facet[0, 1], -facet[0, 0]),
        )
        return turn_parts(((chip * rows_out - P_SIZE // 2 - shift) * along).astype(F32), float(PAD))

    def col_factor(t):
        along = RADIX * iota((8, LANES), 1) + t
        right = iota((8, LANES), 1) < LANES // 2
        upper = iota((8, LANES), 0) < 4
        shift = jnp.where(
            upper,
            jnp.where(right, facet[1, 3], -facet[1, 2]),
            jnp.where(right, facet[1, 1], -facet[1, 0]),
        )
        coef = -(P_SIZE // 2) - shift
        return turn_parts((coef * (along - jnp.where(right, 0, PAD))).astype(F32), float(PAD))

    spot = iota((LANES, LANES), 0)
    row_first = row_factor(LANES, RADIX * spot - jnp.where(spot < LANES // 2, 0, PAD))
    cols = [col_factor(t) for t in range(RADIX)]

    def focal_mask(s):
        factors = [[] for _ in range(RADIX)]
        step = row_factor(8, s)
        for h in range(2):
            rows = slice(h * (LANES // 2), (h + 1) * (LANES // 2))
            row = tuple(part[rows] for part in row_first)
            if s > 0:
                row = times(row, tuple(part[4 * h : 4 * h + 1] for part in step))
            for t in range(RADIX):
                factors[t].append(times(row, tuple(part[4 * h : 4 * h + 1] for part in cols[t])))
        for v in range(RADIX):
            for h in range(2):
                rows = slice(h * (LANES // 2), (h + 1) * (LANES // 2))
                for k, ref in enumerate((mask_c, mask_s)):
                    both = [factors[(2 * v + l) % RADIX][h][k] for l in range(2)]
                    ref[v, s, rows, :] = jnp.concatenate(both, 1).astype(ref.dtype)

    for s in range(1):
        focal_mask(s)

    loads[0].wait()
    lanes = iota((1, LANES), 1)
    for layer in range(layers):
        col = footprint[0, 1, layer]
        far = col >= LANES
        near = col & (LANES - 1)
        frac = fraction[0, 1, layer].astype(F32) / 16.0
        slabs = [screens[layer, :, j * LANES : (j + 1) * LANES] for j in range(4)]
        slabs = [jnp.where(far, slabs[min(j + 1, 3)], slabs[j]) for j in range(4)]
        turn = (LANES - near) & (LANES - 1)
        rolled = [pltpu.roll(slab, turn, 1) for slab in slabs]
        nexts = [pltpu.roll(slab, LANES - 1, 1) for slab in rolled]
        for j in range(3):
            this = jnp.where(lanes < LANES - near, rolled[j], rolled[j + 1])
            after = jnp.where(lanes < LANES - 1 - near, nexts[j], nexts[j + 1])
            value = (1.0 - frac) * this + frac * after
            value_high = value.astype(BF16)
            cut = (slice(layer * band, (layer + 1) * band), slice(j * LANES, (j + 1) * LANES))
            high[cut] = value_high
            low[cut] = (value - value_high.astype(F32)).astype(BF16)

    def partial(which):
        value = dot(pick[which], high[...]) + dot(pick[which], low[...])
        return jnp.round(value * (32768.0 / math.pi)).astype(jnp.int32)

    code = partial(0)
    for t in range(sends):
        snd1[t] = wrapped(code[t * CHUNK : (t + 1) * CHUNK])
    small[3].wait()
    pl.semaphore_wait(barrier, len(peers))
    first = []
    for t in range(sends):
        copy = send(snd1.at[t], rcv1.at[t], s1.at[t], r1.at[t], partner)
        copy.start()
        first.append(copy)
    gather = []
    for k in range(1, m):
        copy = send(tilts.at[0], tilts.at[k], st.at[k - 1], rt.at[k - 1], lax.rem(me + 2 * k, n))
        copy.start()
        gather.append(copy)
    code = partial(1)
    for t in range(sends):
        own[1 + t] = code[t * CHUNK : (t + 1) * CHUNK]
    own[0] = jnp.zeros((CHUNK, WIDE), jnp.int32)
    own[1 + sends] = jnp.zeros((CHUNK, WIDE), jnp.int32)

    second = []
    for t in range(sends):
        first[t].wait()
        total = own[1 + t] + rcv1[t].astype(jnp.int32)
        own[1 + t] = total
        snd2[t] = wrapped(total)
        copies = []
        for k in range(1, m):
            copy = send(
                snd2.at[t], rcv2.at[k - 1, t], s2.at[k - 1, t], r2.at[k - 1, t], lax.rem(me + 2 * k, n)
            )
            copy.start()
            copies.append(copy)
        second.append(copies)
    for s in range(1, RADIX):
        focal_mask(s)

    for load in loads[1:]:
        load.wait()
    for copy in gather:
        copy.wait()
    bases, jumps, acrosses = [], [], []
    for k in range(m):
        for q in range(points):
            steps = tilts[k, q : q + 1, :].astype(F32)
            down, along = steps[:, 0:1], steps[:, 1:2]
            acrosses.append(turn_parts(along * iota((8, WIDE), 1).astype(F32), 8.0 * PAD))
            bases.append(turn_parts(down * iota((CHUNK, LANES), 0).astype(F32), 8.0 * PAD))
            jumps.append(turn_parts(down * (CHUNK * iota((16, LANES), 0)).astype(F32), 8.0 * PAD))
    for which in range(2 * GROUPS):
        for j in range(3):
            cut = slice(j * LANES, (j + 1) * LANES)
            along_y = 2 * (iota((CHUNK, LANES), 0) + which * CHUNK) - P_SIZE + 1
            along_x = 2 * (iota((CHUNK, LANES), 1) + j * LANES) - P_SIZE + 1
            radius = along_y * along_y + along_x * along_x
            edge = P_SIZE * 28 // 100 * (P_SIZE * 28 // 100)
            inside = (radius <= P_SIZE * P_SIZE) & (radius >= edge)
            for p in range(total_points):
                step = tuple(part[which : which + 1] for part in jumps[p])
                col = times(step, tuple(part[0:1, cut] for part in acrosses[p]))
                re, im = times(bases[p], col)
                tilt_c[p, which, :, cut] = jnp.where(inside, re, 0.0)
                tilt_s[p, which, :, cut] = jnp.where(inside, im, 0.0)

    def pupil_piece(code, which):
        field = code_parts(code)
        parts = [[] for _ in range(RADIX)]
        for p in range(total_points):
            pair = []
            for j in range(3):
                cut = slice(j * LANES, (j + 1) * LANES)
                tilt = (tilt_c[p, which, :, cut], tilt_s[p, which, :, cut])
                pair.append(times((field[0][:, cut], field[1][:, cut]), tilt))
            for s, both in enumerate(spread(pair)):
                parts[s].append(jnp.concatenate(both, 1).astype(BF16))
        start_row = pl.multiple_of(which * CHUNK, CHUNK)
        for s in range(RADIX):
            wide = dot(jnp.concatenate(parts[s], 0), flipped[s])
            for p in range(total_points):
                half[p * RADIX + s, pl.ds(start_row, CHUNK), :] = wide[
                    p * CHUNK : (p + 1) * CHUNK
                ].astype(half.dtype)

    shift = 1 - 2 * chip if skip else 0
    third = []
    groups = []

    def pass_on(step, code, group):
        csnd[step] = wrapped(code)
        copy = send(csnd.at[step], crcv.at[step], s3.at[step], r3.at[step], partner)
        copy.start()
        third.append(copy)
        groups.append(group)
        return code

    def from_partner(step):
        third[step].wait()
        return crcv[step].astype(jnp.int32)

    if skip:
        code = pass_on(0, own[1 + 3 * chip], chip * (GROUPS - 1))
        pupil_piece(code, 2 * groups[0] + core)
        pupil_piece(from_partner(0), 2 * groups[0] + other)
    for t in range(sends):
        code = own[1 + t + shift]
        for k in range(1, m):
            second[t][k - 1].wait()
            code = code + rcv2[k - 1, t].astype(jnp.int32)
        step = len(third)
        code = pass_on(step, code, (1 - start if skip else 0) + t)
        last = from_partner(step - 1) if t > 0 else None
        pupil_piece(code, 2 * groups[step] + core)
        if last is not None:
            pupil_piece(last, 2 * groups[step - 1] + other)
    step = len(third) - 1
    pupil_piece(from_partner(step), 2 * groups[step] + other)

    owned = rows_out // 2
    slab = acc.shape[1]
    count = owned // slab
    high_blocks = -(-rows_out // LANES)
    unit = 16
    units = LANES // unit

    def store_back(p, s, first, value):
        row, stop = first, min(first + unit, rows_out)
        while row < stop:
            piece = row // slab
            end = min((piece + 1) * slab, stop)
            back[s, piece, p, row - piece * slab : end - piece * slab, :] = value[row - first : end - first].astype(
                back.dtype
            )
            row = end

    tiles = total_points * RADIX // 2
    work, masked, blocks = (work_a, work_b), (masked_a, masked_b), (blocks_a, blocks_b)

    def paired(ref, s):
        cuts = [slice(k * LANES + i * unit, k * LANES + (i + 1) * unit) for i in range(units) for k in range(2)]
        return jnp.concatenate([ref[s, cut, :] for cut in cuts], 0)

    def spread_unit(t, turn, i):
        count = 3 if (2 * LANES + (i + 1) * unit) <= P_SIZE else 2

        def part(j, k):
            rows = slice(j * LANES + i * unit, j * LANES + (i + 1) * unit)
            return jnp.concatenate(
                [half[2 * t + l, rows, k * LANES : (k + 1) * LANES].astype(F32) for l in range(2)], 1
            )

        for s, pair in enumerate(spread([tuple(part(j, k) for k in range(2)) for j in range(count)])):
            for k in range(2):
                work[turn][s, k * LANES + i * unit : k * LANES + (i + 1) * unit, :] = pair[k].astype(BF16)

    def focal_block(t, turn, s):
        focal = dot(paired(table, s), work[turn][s])
        for i in range(units):
            value = tuple(focal[(2 * i + k) * unit : (2 * i + k + 1) * unit].astype(mask_c.dtype) for k in range(2))
            mask = tuple(ref[t % RADIX, s, i * unit : (i + 1) * unit, :] for ref in (mask_c, mask_s))
            for k, part in enumerate(times(value, mask)):
                masked[turn][s, k * LANES + i * unit : k * LANES + (i + 1) * unit, :] = part.astype(BF16)

    def back_block(turn, s):
        blocks[turn][s] = dot(paired(flipped, s), masked[turn][s])

    def gather_unit(t, turn, i):
        z = [
            tuple(blocks[turn][s, (2 * i + k) * unit : (2 * i + k + 1) * unit, :] for k in range(2))
            for s in range(RADIX)
        ]
        wanted = [a for a in range(high_blocks) if a * LANES + i * unit < rows_out]
        for a, pair in zip(wanted, gather_blocks(z, wanted)):
            for l in range(2):
                p, v = (2 * t + l) // RADIX, (2 * t + l) % RADIX
                cut = slice(l * LANES, (l + 1) * LANES)
                store_back(p, v, a * LANES + i * unit, jnp.concatenate([part[:, cut] for part in pair], 1))

    shares = [range((units * s) // RADIX, (units * (s + 1)) // RADIX) for s in range(RADIX)]

    def step(t, turn, spreads=True, focals=True, backs=True, gathers=True):
        for s in range(RADIX):
            if focals:
                focal_block(t, turn, s)
            if backs:
                back_block(1 - turn, s)
            for i in shares[s]:
                if spreads:
                    spread_unit(t + 1, 1 - turn, i)
                if gathers:
                    gather_unit(t - 2, turn, i)

    def two_steps(i, carry):
        step(2 * i + 3, 1)
        step(2 * i + 4, 0)
        return carry

    for i in range(units):
        spread_unit(0, 0, i)
    step(0, 0, backs=False, gathers=False)
    step(1, 1, gathers=False)
    step(2, 0)
    if tiles <= 16:
        for i in range((tiles - 4) // 2):
            two_steps(i, 0)
    else:
        lax.fori_loop(0, (tiles - 4) // 2, two_steps, 0)
    step(tiles - 1, 1, spreads=False)
    step(tiles, 0, spreads=False, focals=False)
    step(tiles + 1, 1, spreads=False, focals=False, backs=False)

    def image_block(piece, turn, s):
        rows = back[s, piece].reshape(total_points * slab, SPLIT)
        wide[turn % 2, s] = dot(rows.astype(BF16), table[s])

    def image_rows(turn, row, dst, c):
        sums = [None] * RADIX
        for p in range(total_points):
            rows = slice(p * slab + row, p * slab + row + 8)
            z = [tuple(wide[turn % 2, s, rows, k * LANES : (k + 1) * LANES] for k in range(2)) for s in range(RADIX)]
            for j, (re, im) in enumerate(gather_blocks(z, list(range(RADIX)))):
                power = re * re + im * im
                sums[j] = power if p == 0 else sums[j] + power
        for j in range(RADIX):
            dst[c, row : row + 8, j * LANES : (j + 1) * LANES] = sums[j]

    fourth = []
    pieces = [(other * count + c, isnd, c) for c in range(count)] + [(core * count + c, acc, c) for c in range(count)]
    for turn in range(len(pieces) + 1):
        for s in range(RADIX):
            if turn < len(pieces):
                image_block(pieces[turn][0], turn, s)
            if turn > 0:
                _, dst, c = pieces[turn - 1]
                rows = list(range(0, slab, 8))
                for row in rows[(len(rows) * s) // RADIX : (len(rows) * (s + 1)) // RADIX]:
                    image_rows(turn - 1, row, dst, c)
        if 0 < turn <= count:
            c = turn - 1
            copy = send(isnd.at[c], ircv.at[c], s4.at[c], r4.at[c], partner)
            copy.start()
            fourth.append(copy)
    for c in range(count):
        fourth[c].wait()
        out[0, c * slab : (c + 1) * slab, :] = acc[c] + ircv[c]


def solution(mesh):
    n = mesh.shape["mod"]
    m = n // 2
    owned = PAD // n
    slab = 80 if owned % 80 == 0 else owned
    consts = tables()

    def shards(screens, footprint, fraction, tilt_steps, facet_shift):
        layers, band, width = screens.shape
        points = tilt_steps.shape[0]
        total = points * m
        reach = 2 * CHUNK * (GROUPS - 1)
        skip = m == 2 and 2 * band <= reach and 2 * band - (width - P_SIZE) >= P_SIZE - reach
        sends = GROUPS - 1 if skip else GROUPS
        vmem = pl.BlockSpec(memory_space=pltpu.VMEM)
        hbm = pl.BlockSpec(memory_space=pltpu.HBM)
        dma = pltpu.SemaphoreType.DMA
        codes = lambda count, kind: pltpu.VMEM((count, CHUNK, WIDE), kind)
        detector = pl.pallas_call(
            functools.partial(kernel, n, layers, band, points, skip),
            out_shape=pltpu.VMEM((1, owned, PAD), F32),
            in_specs=[hbm] * 7,
            out_specs=vmem,
            scratch_shapes=[
                pltpu.SMEM((1, 2, layers), jnp.int32),
                pltpu.SMEM((1, 2, layers), jnp.int32),
                pltpu.VMEM((m, points, 2), jnp.int32),
                pltpu.SMEM(facet_shift.shape[::-1], jnp.int32),
                pltpu.VMEM((layers, band, width), F32),
                pltpu.VMEM((RADIX, SPLIT, SPLIT), BF16),
                pltpu.VMEM((RADIX, SPLIT, SPLIT), BF16),
                pltpu.VMEM((2, sends * CHUNK, layers * band), BF16),
                pltpu.VMEM((layers * band, WIDE), BF16),
                pltpu.VMEM((layers * band, WIDE), BF16),
                codes(sends + 2, jnp.int32),
                codes(sends, jnp.int16),
                codes(sends, jnp.int16),
                codes(sends, jnp.int16),
                pltpu.VMEM((m - 1, sends, CHUNK, WIDE), jnp.int16),
                codes(GROUPS, jnp.int16),
                codes(GROUPS, jnp.int16),
                pltpu.VMEM((total, 2 * GROUPS, CHUNK, WIDE), F32),
                pltpu.VMEM((total, 2 * GROUPS, CHUNK, WIDE), F32),
                pltpu.VMEM((RADIX, RADIX, LANES, SPLIT), BF16),
                pltpu.VMEM((RADIX, RADIX, LANES, SPLIT), BF16),
                pltpu.VMEM((total * RADIX, P_SIZE, SPLIT), F32 if total <= 8 else BF16),
                pltpu.VMEM((RADIX, SPLIT, SPLIT), BF16),
                pltpu.VMEM((RADIX, SPLIT, SPLIT), BF16),
                pltpu.VMEM((RADIX, SPLIT, SPLIT), BF16),
                pltpu.VMEM((RADIX, SPLIT, SPLIT), BF16),
                pltpu.VMEM((RADIX, SPLIT, SPLIT), F32),
                pltpu.VMEM((RADIX, SPLIT, SPLIT), F32),
                pltpu.VMEM((2, RADIX, total * slab, SPLIT), F32),
                pltpu.VMEM((RADIX, 2 * owned // slab, total, slab, SPLIT), BF16 if slab % 16 == 0 else F32),
                pltpu.VMEM((owned // slab, slab, PAD), F32),
                pltpu.VMEM((owned // slab, slab, PAD), F32),
                pltpu.VMEM((owned // slab, slab, PAD), F32),
                dma((4,)),
                dma((3,)),
                dma((m - 1,)), dma((m - 1,)),
                dma((sends,)), dma((sends,)),
                dma((m - 1, sends)), dma((m - 1, sends)),
                dma((GROUPS,)), dma((GROUPS,)),
                dma((owned // slab,)), dma((owned // slab,)),
            ],
            compiler_params=pltpu.CompilerParams(
                collective_id=0, has_side_effects=True, vmem_limit_bytes=60 * 1024 * 1024
            ),
        )(footprint.swapaxes(1, 2), fraction.swapaxes(1, 2), tilt_steps, facet_shift.T, screens, *[jnp.asarray(t) for t in consts])
        return detector * (4.0 / (points * n))

    placed = (
        P("group", "mod", None),
        P(("group", "dir"), None, None),
        P(("group", "dir"), None, None),
        P(("group", "mod"), None),
        P(),
    )
    return jax.shard_map(
        shards,
        mesh=mesh,
        in_specs=placed,
        out_specs=P(("group", "dir"), "mod", None),
        check_vma=False,
    )
```

time: 24.9 us -> 22.5 us (0.904)
  Pallas kernels: 22.9 us -> 21.5 us
  other arithmetic: 1.78 us -> 0.78 us
    pallas_call x1, Pallas kernels: 22.9 us -> 21.5 us  [shards(): pl.pallas_call(functools.partial(kernel, n, layers, band, points, skip),...]
    mul x1, other arithmetic: 1.78 us -> 0.78 us  [shards(): return detector * (4.0 / (points * n))]
where the time goes in v2:
time: 22.5 us; the launch traced here: 22.3 us
  Pallas kernels  21.5 us (96%)
  other arithmetic  0.78 us (3%)
    pallas_call x1, Pallas kernels, shards(): pl.pallas_call(functools.partial(kernel, n, layers, band, points, skip),...  21.5 us
    mul x1, other arithmetic, shards(): return detector * (4.0 / (points * n))  0.78 us

profile of v2, /device:TPU:0, one launch (start us, length us, event | category | flops | bytes accessed | tf_op | source)
XLA Modules:
  0.0 22.3 jit_solution(131401838160662310)
XLA Ops:
  0.0 21.5 %shard_map.73 = f32[1,160,640]{2,1,0:T(8,128)S(1)} custom-call(s32[1,2,4]{2,1,0:T(2,128)} %bitcast.3, s32[1,2,4]{2,1,0:T(2,128)} %bitcast.4, s32[2,2]{1,0:T(2,128)} %tilt_hbm.1, s32[2,4]{1,0:T(2,128)} %bitcast.5, f32[4,128,512]{2,1,0:T(8,128)} %screens_hbm.1, bf16[5,256,256]{2,1,0:T(8,128)(2,1)} %constant.6.clone.table_hbm, ...), custom_call_target="tpu_custom_call" | custom-call | tf_op jit(solution)/shard_map/pallas_call | solution.py:530
  21.6 0.8 %broadcast_multiply_fusion = f32[1,160,640]{2,1,0:T(8,128)} fusion(f32[1,160,640]{2,1,0:T(8,128)S(1)} %shard_map.73), kind=kLoop, calls=%fused_computation | loop fusion | flops 102400 | bytes 819200 | tf_op jit(solution)/shard_map/mul | solution.py:581

commit v3 on v2

--- a/solution.py
+++ b/solution.py
@@ -15,6 +15,7 @@
 RADIX = PAD // LANES
 WIDE = 384
 CHUNK = 32
+FINE = 16
 GROUPS = P_SIZE // (2 * CHUNK)
 SPLIT = 2 * LANES
 MESH = pl.DeviceIdType.MESH
@@ -328,23 +329,34 @@
                 tilt_s[p, which, :, cut] = jnp.where(inside, im, 0.0)
 
     def pupil_piece(code, which):
-        field = code_parts(code)
-        parts = [[] for _ in range(RADIX)]
-        for p in range(total_points):
-            pair = []
-            for j in range(3):
-                cut = slice(j * LANES, (j + 1) * LANES)
-                tilt = (tilt_c[p, which, :, cut], tilt_s[p, which, :, cut])
-                pair.append(times((field[0][:, cut], field[1][:, cut]), tilt))
-            for s, both in enumerate(spread(pair)):
-                parts[s].append(jnp.concatenate(both, 1).astype(BF16))
+        parts = [[[] for _ in range(total_points)] for _ in range(RADIX)]
+        cuts = [slice(j * LANES, (j + 1) * LANES) for j in range(3)]
+        for first in range(0, CHUNK, 16):
+            fresh = [[[] for _ in range(total_points)] for _ in range(RADIX)]
+            for top in range(first, first + 16, 8):
+                rows = slice(top, top + 8)
+                field = [code_parts(code[rows, cut]) for cut in cuts]
+                for p in range(total_points):
+                    tilted = [
+                        times(field[j], (tilt_c[p, which, rows, cuts[j]], tilt_s[p, which, rows, cuts[j]]))
+                        for j in range(3)
+                    ]
+                    for s, both in enumerate(spread(tilted)):
+                        fresh[s][p].append(jnp.concatenate(both, 1))
+            for s in range(RADIX):
+                for p in range(total_points):
+                    parts[s][p].append(jnp.concatenate(fresh[s][p], 0).astype(BF16))
         start_row = pl.multiple_of(which * CHUNK, CHUNK)
-        for s in range(RADIX):
-            wide = dot(jnp.concatenate(parts[s], 0), flipped[s])
-            for p in range(total_points):
-                half[p * RADIX + s, pl.ds(start_row, CHUNK), :] = wide[
-                    p * CHUNK : (p + 1) * CHUNK
-                ].astype(half.dtype)
+        wides = [
+            dot(jnp.concatenate([one for rows in parts[s] for one in rows], 0), flipped[s]) for s in range(RADIX)
+        ]
+        for t in range(total_points * RADIX // 2):
+            for k in range(2):
+                both = []
+                for block in (2 * t, 2 * t + 1):
+                    p, s = block // RADIX, block % RADIX
+                    both.append(wides[s][p * CHUNK : (p + 1) * CHUNK, k * LANES : (k + 1) * LANES])
+                half[t, k, pl.ds(start_row, CHUNK), :] = jnp.concatenate(both, 1).astype(BF16)
 
     shift = 1 - 2 * chip if skip else 0
     third = []
@@ -388,7 +400,7 @@
     units = LANES // unit
 
     def store_back(p, s, first, value):
-        row, stop = first, min(first + unit, rows_out)
+        row, stop = first, min(first + FINE, rows_out)
         while row < stop:
             piece = row // slab
             end = min((piece + 1) * slab, stop)
@@ -406,16 +418,14 @@
 
     def spread_unit(t, turn, i):
         count = 3 if (2 * LANES + (i + 1) * unit) <= P_SIZE else 2
-
-        def part(j, k):
-            rows = slice(j * LANES + i * unit, j * LANES + (i + 1) * unit)
-            return jnp.concatenate(
-                [half[2 * t + l, rows, k * LANES : (k + 1) * LANES].astype(F32) for l in range(2)], 1
-            )
-
-        for s, pair in enumerate(spread([tuple(part(j, k) for k in range(2)) for j in range(count)])):
-            for k in range(2):
-                work[turn][s, k * LANES + i * unit : k * LANES + (i + 1) * unit, :] = pair[k].astype(BF16)
+        for first in range(i * unit, (i + 1) * unit, FINE):
+
+            def part(j, k):
+                return half[t, k, j * LANES + first : j * LANES + first + FINE, :]
+
+            for s, pair in enumerate(spread([tuple(part(j, k) for k in range(2)) for j in range(count)])):
+                for k in range(2):
+                    work[turn][s, k * LANES + first : k * LANES + first + FINE, :] = pair[k].astype(BF16)
 
     def focal_block(t, turn, s):
         focal = dot(paired(table, s), work[turn][s])
@@ -429,16 +439,17 @@
         blocks[turn][s] = dot(paired(flipped, s), masked[turn][s])
 
     def gather_unit(t, turn, i):
-        z = [
-            tuple(blocks[turn][s, (2 * i + k) * unit : (2 * i + k + 1) * unit, :] for k in range(2))
-            for s in range(RADIX)
-        ]
-        wanted = [a for a in range(high_blocks) if a * LANES + i * unit < rows_out]
-        for a, pair in zip(wanted, gather_blocks(z, wanted)):
-            for l in range(2):
-                p, v = (2 * t + l) // RADIX, (2 * t + l) % RADIX
-                cut = slice(l * LANES, (l + 1) * LANES)
-                store_back(p, v, a * LANES + i * unit, jnp.concatenate([part[:, cut] for part in pair], 1))
+        for first in range(i * unit, (i + 1) * unit, FINE):
+            z = []
+            for s in range(RADIX):
+                starts = [2 * i * unit + k * unit + first - i * unit for k in range(2)]
+                z.append(tuple(blocks[turn][s, start : start + FINE, :] for start in starts))
+            wanted = [a for a in range(high_blocks) if a * LANES + first < rows_out]
+            for a, pair in zip(wanted, gather_blocks(z, wanted)):
+                for l in range(2):
+                    p, v = (2 * t + l) // RADIX, (2 * t + l) % RADIX
+                    cut = slice(l * LANES, (l + 1) * LANES)
+                    store_back(p, v, a * LANES + first, jnp.concatenate([part[:, cut] for part in pair], 1))
 
     shares = [range((units * s) // RADIX, (units * (s + 1)) // RADIX) for s in range(RADIX)]
 
@@ -554,7 +565,7 @@
                 pltpu.VMEM((total, 2 * GROUPS, CHUNK, WIDE), F32),
                 pltpu.VMEM((RADIX, RADIX, LANES, SPLIT), BF16),
                 pltpu.VMEM((RADIX, RADIX, LANES, SPLIT), BF16),
-                pltpu.VMEM((total * RADIX, P_SIZE, SPLIT), F32 if total <= 8 else BF16),
+                pltpu.VMEM((total * RADIX // 2, 2, P_SIZE, SPLIT), BF16),
                 pltpu.VMEM((RADIX, SPLIT, SPLIT), BF16),
                 pltpu.VMEM((RADIX, SPLIT, SPLIT), BF16),
                 pltpu.VMEM((RADIX, SPLIT, SPLIT), BF16),

time: 22.5 us -> 21.6 us (0.960)
  Pallas kernels: 21.5 us -> 20.6 us
    pallas_call x1, Pallas kernels: 21.5 us -> 20.6 us  [shards(): pl.pallas_call(functools.partial(kernel, n, layers, band, points, skip),...]
where the time goes in v3:
time: 21.6 us; the launch traced here: 21.4 us
  Pallas kernels  20.6 us (95%)
  other arithmetic  0.78 us (4%)
    pallas_call x1, Pallas kernels, shards(): pl.pallas_call(functools.partial(kernel, n, layers, band, points, skip),...  20.6 us
    mul x1, other arithmetic, shards(): return detector * (4.0 / (points * n))  0.78 us

profile of v3, /device:TPU:0, one launch (start us, length us, event | category | flops | bytes accessed | tf_op | source)
XLA Modules:
  0.0 21.4 jit_solution(8895315700314441118)
XLA Ops:
  0.0 20.6 %shard_map.73 = f32[1,160,640]{2,1,0:T(8,128)S(1)} custom-call(s32[1,2,4]{2,1,0:T(2,128)} %bitcast.3, s32[1,2,4]{2,1,0:T(2,128)} %bitcast.4, s32[2,2]{1,0:T(2,128)} %tilt_hbm.1, s32[2,4]{1,0:T(2,128)} %bitcast.5, f32[4,128,512]{2,1,0:T(8,128)} %screens_hbm.1, bf16[5,256,256]{2,1,0:T(8,128)(2,1)} %constant.6.clone.table_hbm, ...), custom_call_target="tpu_custom_call" | custom-call | tf_op jit(solution)/shard_map/pallas_call | solution.py:541
  20.6 0.8 %broadcast_multiply_fusion = f32[1,160,640]{2,1,0:T(8,128)} fusion(f32[1,160,640]{2,1,0:T(8,128)S(1)} %shard_map.73), kind=kLoop, calls=%fused_computation | loop fusion | flops 102400 | bytes 819200 | tf_op jit(solution)/shard_map/mul | solution.py:592

commit v4 on v3

--- a/solution.py
+++ b/solution.py
@@ -15,6 +15,7 @@
 RADIX = PAD // LANES
 WIDE = 384
 CHUNK = 32
+PACKED = CHUNK + 8
 FINE = 16
 GROUPS = P_SIZE // (2 * CHUNK)
 SPLIT = 2 * LANES
@@ -69,6 +70,21 @@
     cos_out = jnp.where(((index + 1) & 2) == 2, -cos_out, cos_out)
     sin_out = jnp.where((index & 2) == 2, -sin_out, sin_out)
     return cos_out, sin_out
+
+
+def pack_codes(code):
+    low = iota((8, LANES), 1) < LANES // 2
+    last = [code[k : k + 8, 2 * LANES :] for k in range(0, CHUNK, 8)]
+    folded = [jnp.where(low, last[k], pltpu.roll(last[k + 1], LANES // 2, 1)) for k in (0, 2)]
+    return jnp.concatenate([code[:, : 2 * LANES], jnp.concatenate(folded, 1)], 0)
+
+
+def code_block(packed, top, j):
+    if j < 2:
+        return packed[top : top + 8, j * LANES : (j + 1) * LANES]
+    k = top // 8
+    block = packed[CHUNK:PACKED, (k // 2) * LANES : (k // 2 + 1) * LANES]
+    return pltpu.roll(block, LANES // 2, 1) if k % 2 else block
 
 
 def iota(shape, axis):
@@ -265,7 +281,7 @@
 
     code = partial(0)
     for t in range(sends):
-        snd1[t] = wrapped(code[t * CHUNK : (t + 1) * CHUNK])
+        snd1[t] = wrapped(pack_codes(code[t * CHUNK : (t + 1) * CHUNK]))
     small[3].wait()
     pl.semaphore_wait(barrier, len(peers))
     first = []
@@ -280,9 +296,9 @@
         gather.append(copy)
     code = partial(1)
     for t in range(sends):
-        own[1 + t] = code[t * CHUNK : (t + 1) * CHUNK]
-    own[0] = jnp.zeros((CHUNK, WIDE), jnp.int32)
-    own[1 + sends] = jnp.zeros((CHUNK, WIDE), jnp.int32)
+        own[1 + t] = pack_codes(code[t * CHUNK : (t + 1) * CHUNK])
+    own[0] = jnp.zeros((PACKED, SPLIT), jnp.int32)
+    own[1 + sends] = jnp.zeros((PACKED, SPLIT), jnp.int32)
 
     second = []
     for t in range(sends):
@@ -335,7 +351,7 @@
             fresh = [[[] for _ in range(total_points)] for _ in range(RADIX)]
             for top in range(first, first + 16, 8):
                 rows = slice(top, top + 8)
-                field = [code_parts(code[rows, cut]) for cut in cuts]
+                field = [code_parts(code_block(code, top, j)) for j in range(3)]
                 for p in range(total_points):
                     tilted = [
                         times(field[j], (tilt_c[p, which, rows, cuts[j]], tilt_s[p, which, rows, cuts[j]]))
@@ -347,6 +363,12 @@
                 for p in range(total_points):
                     parts[s][p].append(jnp.concatenate(fresh[s][p], 0).astype(BF16))
         start_row = pl.multiple_of(which * CHUNK, CHUNK)
+        def products():
+            return finish_piece(parts, start_row)
+
+        return products
+
+    def finish_piece(parts, start_row):
         wides = [
             dot(jnp.concatenate([one for rows in parts[s] for one in rows], 0), flipped[s]) for s in range(RADIX)
         ]
@@ -374,10 +396,21 @@
         third[step].wait()
         return crcv[step].astype(jnp.int32)
 
+    ready = []
+
+    def prepare(code, which):
+        ready.append(pupil_piece(code, which))
+
+    def flush(keep):
+        while len(ready) > keep:
+            ready.pop(0)()
+
     if skip:
         code = pass_on(0, own[1 + 3 * chip], chip * (GROUPS - 1))
-        pupil_piece(code, 2 * groups[0] + core)
-        pupil_piece(from_partner(0), 2 * groups[0] + other)
+        prepare(code, 2 * groups[0] + core)
+        last = from_partner(0)
+        flush(0)
+        prepare(last, 2 * groups[0] + other)
     for t in range(sends):
         code = own[1 + t + shift]
         for k in range(1, m):
@@ -386,11 +419,15 @@
         step = len(third)
         code = pass_on(step, code, (1 - start if skip else 0) + t)
         last = from_partner(step - 1) if t > 0 else None
-        pupil_piece(code, 2 * groups[step] + core)
+        flush(0)
+        prepare(code, 2 * groups[step] + core)
         if last is not None:
-            pupil_piece(last, 2 * groups[step - 1] + other)
+            prepare(last, 2 * groups[step - 1] + other)
     step = len(third) - 1
-    pupil_piece(from_partner(step), 2 * groups[step] + other)
+    last = from_partner(step)
+    flush(0)
+    prepare(last, 2 * groups[step] + other)
+    flush(0)
 
     owned = rows_out // 2
     slab = acc.shape[1]
@@ -497,7 +534,7 @@
                 power = re * re + im * im
                 sums[j] = power if p == 0 else sums[j] + power
         for j in range(RADIX):
-            dst[c, row : row + 8, j * LANES : (j + 1) * LANES] = sums[j]
+            dst[c, row : row + 8, j * LANES : (j + 1) * LANES] = sums[j].astype(dst.dtype)
 
     fourth = []
     pieces = [(other * count + c, isnd, c) for c in range(count)] + [(core * count + c, acc, c) for c in range(count)]
@@ -517,7 +554,7 @@
             fourth.append(copy)
     for c in range(count):
         fourth[c].wait()
-        out[0, c * slab : (c + 1) * slab, :] = acc[c] + ircv[c]
+        out[0, c * slab : (c + 1) * slab, :] = acc[c] + ircv[c].astype(F32)
 
 
 def solution(mesh):
@@ -537,7 +574,7 @@
         vmem = pl.BlockSpec(memory_space=pltpu.VMEM)
         hbm = pl.BlockSpec(memory_space=pltpu.HBM)
         dma = pltpu.SemaphoreType.DMA
-        codes = lambda count, kind: pltpu.VMEM((count, CHUNK, WIDE), kind)
+        codes = lambda count, kind: pltpu.VMEM((count, PACKED, SPLIT), kind)
         detector = pl.pallas_call(
             functools.partial(kernel, n, layers, band, points, skip),
             out_shape=pltpu.VMEM((1, owned, PAD), F32),
@@ -558,7 +595,7 @@
                 codes(sends, jnp.int16),
                 codes(sends, jnp.int16),
                 codes(sends, jnp.int16),
-                pltpu.VMEM((m - 1, sends, CHUNK, WIDE), jnp.int16),
+                pltpu.VMEM((m - 1, sends, PACKED, SPLIT), jnp.int16),
                 codes(GROUPS, jnp.int16),
                 codes(GROUPS, jnp.int16),
                 pltpu.VMEM((total, 2 * GROUPS, CHUNK, WIDE), F32),
@@ -575,8 +612,8 @@
                 pltpu.VMEM((2, RADIX, total * slab, SPLIT), F32),
                 pltpu.VMEM((RADIX, 2 * owned // slab, total, slab, SPLIT), BF16 if slab % 16 == 0 else F32),
                 pltpu.VMEM((owned // slab, slab, PAD), F32),
-                pltpu.VMEM((owned // slab, slab, PAD), F32),
-                pltpu.VMEM((owned // slab, slab, PAD), F32),
+                pltpu.VMEM((owned // slab, slab, PAD), BF16),
+                pltpu.VMEM((owned // slab, slab, PAD), BF16),
                 dma((4,)),
                 dma((3,)),
                 dma((m - 1,)), dma((m - 1,)),

time: 21.6 us -> 21.4 us (level)
  no operation moved by 1% of the time
where the time goes in v4:
time: 21.4 us; the launch traced here: 21.3 us
  Pallas kernels  20.5 us (96%)
  other arithmetic  0.78 us (4%)
    pallas_call x1, Pallas kernels, shards(): pl.pallas_call(functools.partial(kernel, n, layers, band, points, skip),...  20.5 us
    mul x1, other arithmetic, shards(): return detector * (4.0 / (points * n))  0.78 us

profile of v4, /device:TPU:0, one launch (start us, length us, event | category | flops | bytes accessed | tf_op | source)
XLA Modules:
  0.0 21.3 jit_solution(13521875029370395870)
XLA Ops:
  0.0 20.5 %shard_map.73 = f32[1,160,640]{2,1,0:T(8,128)S(1)} custom-call(s32[1,2,4]{2,1,0:T(2,128)} %bitcast.3, s32[1,2,4]{2,1,0:T(2,128)} %bitcast.4, s32[2,2]{1,0:T(2,128)} %tilt_hbm.1, s32[2,4]{1,0:T(2,128)} %bitcast.5, f32[4,128,512]{2,1,0:T(8,128)} %screens_hbm.1, bf16[5,256,256]{2,1,0:T(8,128)(2,1)} %constant.6.clone.table_hbm, ...), custom_call_target="tpu_custom_call" | custom-call | tf_op jit(solution)/shard_map/pallas_call | solution.py:578
  20.5 0.8 %broadcast_multiply_fusion = f32[1,160,640]{2,1,0:T(8,128)} fusion(f32[1,160,640]{2,1,0:T(8,128)S(1)} %shard_map.73), kind=kLoop, calls=%fused_computation | loop fusion | flops 102400 | bytes 819200 | tf_op jit(solution)/shard_map/mul | solution.py:629
